TPU v7x, 256 devices: a whole 4x4x8 slice. The times are simulated.
256 devices in a mesh: panel: 8 (over x, core), front: 32 (over z, y).
Axes of the slice: x: 4, y: 4, z: 8, core: 2. Of those that a mesh axis runs over, the one named last changes fastest.
Arguments:
- rhs: float32 [8, 64, 64, 2, 128], P('panel', None, 'front'), may hold values from -6 to 6
- fronts: bfloat16 [8, 2, 8192, 8192], P('panel', None, 'front'), may hold values from -0.046875 to 0.046875
- wave_sq: float32 [8, 64, 128], P('panel', 'front'), may hold values from 0.5 to 2
- pml_width: int32 [8], P('panel'), may hold values from 1 to 16
Outputs:
- sweep_field: float32 [8, 64, 64, 2, 128], P('panel', None, 'front')
- residual: float32 [8, 64, 64, 2, 128], P('panel', None, 'front')
All inputs are finite; a program needn't handle non-finite values.
Results may differ from a plain program's by a relative error of at most 0.013.
Values may be sent and summed in bfloat16 or wider, within the bound.
A program may use at most 64 MiB of HBM per device.

v0:
```python
import jax
import jax.numpy as jnp
from jax import lax
from jax.sharding import PartitionSpec as P


def from_behind(shard, axis, by):
    devices = lax.axis_size(axis)
    pairs = [(i, i + by) for i in range(devices) if 0 <= i + by < devices]
    return lax.ppermute(shard, axis, pairs)


def padded_2(cells, sides, width):
    for axis, dim in sides:
        count = lax.axis_size(axis)
        ends = count - 1
        head = lax.slice_in_dim(cells, 0, width, axis=dim)
        tail = lax.slice_in_dim(cells, cells.shape[dim] - width, cells.shape[dim], axis=dim)
        cells = jnp.concatenate(
            [
                lax.ppermute(tail, axis, [(i, (i + 1) % count) for i in range(ends)]),
                cells,
                lax.ppermute(head, axis, [((i + 1) % count, i) for i in range(ends)]),
            ],
            axis=dim,
        )
    return cells


def local(rhs, fronts, wave_sq, pml_width):
    group_panels, rhs_count, row_count, components, columns = rhs.shape
    panel_count = lax.axis_size("panel")
    group_index = lax.axis_index("panel")
    block_count = 1
    block_size = rhs_count // block_count

    def apply_front(combined, local_panel):
        front_re = fronts[local_panel, 0]
        front_im = fronts[local_panel, 1]
        vector_piece = lax.all_gather(combined, "front", axis=1, tiled=True)
        piece_rows = vector_piece.shape[1]
        width = piece_rows * columns
        part_re = vector_piece[:, :, 0].reshape(block_size, width)
        part_im = vector_piece[:, :, 1].reshape(block_size, width)
        dims = (((1,), (1,)), ((), ()))
        new_re = lax.dot_general(
            part_re, front_re, dims, preferred_element_type=jnp.float32
        ) - lax.dot_general(part_im, front_im, dims, preferred_element_type=jnp.float32)
        new_im = lax.dot_general(
            part_re, front_im, dims, preferred_element_type=jnp.float32
        ) + lax.dot_general(part_im, front_re, dims, preferred_element_type=jnp.float32)
        return jnp.stack(
            [
                new_re.reshape(block_size, row_count, columns),
                new_im.reshape(block_size, row_count, columns),
            ],
            axis=2,
        )

    def one_section(section_num, carry):
        solved_all, incoming = carry
        block_num = section_num - group_index
        active = (block_num >= 0) & (block_num < block_count)
        previous = incoming
        rhs_block = rhs[0]
        combined = (rhs_block + previous).astype(jnp.bfloat16)
        solved = apply_front(combined, 0)
        earlier = solved_all
        solved_all = jnp.where(active, solved[None], earlier)
        incoming = from_behind(solved, "panel", 1)
        return (solved_all, incoming)

    start_all = jnp.zeros(rhs.shape, jnp.float32)
    start_in = jnp.zeros((block_size, row_count, components, columns), jnp.float32)
    sweep_field, _ = lax.fori_loop(
        0, panel_count + block_count - 1, one_section, (start_all, start_in)
    )
    padded = padded_2(sweep_field.astype(jnp.bfloat16), (("panel", 0), ("front", 2)), 1).astype(
        sweep_field.dtype
    )
    beside = padded[2:, :, 1:-1] + padded[:-2, :, 1:-1]
    beside = beside + padded[1:-1, :, 2:] + padded[1:-1, :, :-2]
    side_pad = jnp.pad(sweep_field, ((0, 0), (0, 0), (0, 0), (0, 0), (1, 1)))
    beside = beside + side_pad[..., 2:] + side_pad[..., :-2]
    plane_rows = lax.axis_index("front") * row_count + jnp.arange(row_count, dtype=jnp.int32)
    row_pos = plane_rows.astype(jnp.float32)[None, :]
    total_rows = row_count * lax.axis_size("front")
    thick = pml_width.astype(jnp.float32)[:, None]
    absorb = (
        2.0
        * (jnp.maximum(0.0, thick - row_pos) + jnp.maximum(0.0, row_pos - (total_rows - 1 - thick)))
        / thick
    )
    absorb_b = absorb[:, None, :, None]
    diagonal_term = (6.0 - wave_sq)[:, None, :, :]
    real_part = sweep_field[:, :, :, 0]
    imag_part = sweep_field[:, :, :, 1]
    apply_re = diagonal_term * real_part - absorb_b * imag_part - beside[:, :, :, 0]
    apply_im = diagonal_term * imag_part + absorb_b * real_part - beside[:, :, :, 1]
    residual = rhs - jnp.stack([apply_re, apply_im], axis=3)
    return (sweep_field, residual)


def solution(mesh):
    return jax.shard_map(
        local,
        mesh=mesh,
        in_specs=(
            P("panel", None, "front", None, None),
            P("panel", None, "front", None),
            P("panel", "front", None),
            P("panel"),
        ),
        out_specs=(P("panel", None, "front", None, None), P("panel", None, "front", None, None)),
        check_vma=False,
    )
```

profile of v0, /device:TPU:29, one launch (start us, length us, event | category | flops | bytes accessed | tf_op | source)
XLA Modules:
  0.0 821.7 jit_solution(15315599184756848549)
XLA Ops:
  8.2 782.1 %while.16 = (s32[]{:T(128)}, f32[1,64,2,2,128]{4,2,1,3,0:T(2,128)S(1)}, f32[64,2,2,128]{3,1,0,2:T(2,128)S(1)}, s32[]{:T(128)}, f32[1,64,2,2,128]{4,1,3,2,0:T(8,1...) while((s32[]{:T(128)}, f32[1,64,2,2,128]{4,2,1,3,0:T(2,128)S(1)}, ...), condition=%wide.region_1.2_spmd.clone, body=%wide.region_0.1_spmd.clone.sunk | while | flops 1073905664 | bytes 71565536 | solution.py:75
  8.9 78.8 %all-gather.2.cloned.1.call-done = bf16[64,64,2,128]{3,0,2,1:T(8,128)(2,1)} async-done(((bf16[64,2,2,128]{3,0,2,1:T(8,128)(2,1)}), bf16[64,64,2,128]{3,0,2,1:T(8,128)(2,1)}) %all-gather.2.cloned.1.call-update) | async-done | bytes 2097168 | tf_op jit(solution)/shard_map/while/body/eval_jaxpr/all_gather | solution.py:40
  96.0 3.7 fusion.58
  99.8 7.0 collective-permute-start
  109.4 75.8 %all-gather.2.cloned.1.call-done = bf16[64,64,2,128]{3,0,2,1:T(8,128)(2,1)} async-done(((bf16[64,2,2,128]{3,0,2,1:T(8,128)(2,1)}), bf16[64,64,2,128]{3,0,2,1:T(8,128)(2,1)}) %all-gather.2.cloned.1.call-update) | async-done | bytes 2097168 | tf_op jit(solution)/shard_map/while/body/eval_jaxpr/all_gather | solution.py:40
  193.5 3.7 fusion.58
  197.3 7.0 collective-permute-start
  206.9 75.8 %all-gather.2.cloned.1.call-done = bf16[64,64,2,128]{3,0,2,1:T(8,128)(2,1)} async-done(((bf16[64,2,2,128]{3,0,2,1:T(8,128)(2,1)}), bf16[64,64,2,128]{3,0,2,1:T(8,128)(2,1)}) %all-gather.2.cloned.1.call-update) | async-done | bytes 2097168 | tf_op jit(solution)/shard_map/while/body/eval_jaxpr/all_gather | solution.py:40
  294.8 7.0 collective-permute-start
  304.4 75.5 %all-gather.2.cloned.1.call-done = bf16[64,64,2,128]{3,0,2,1:T(8,128)(2,1)} async-done(((bf16[64,2,2,128]{3,0,2,1:T(8,128)(2,1)}), bf16[64,64,2,128]{3,0,2,1:T(8,128)(2,1)}) %all-gather.2.cloned.1.call-update) | async-done | bytes 2097168 | tf_op jit(solution)/shard_map/while/body/eval_jaxpr/all_gather | solution.py:40
  388.2 3.7 fusion.58
  391.9 7.0 collective-permute-start
  401.6 75.5 %all-gather.2.cloned.1.call-done = bf16[64,64,2,128]{3,0,2,1:T(8,128)(2,1)} async-done(((bf16[64,2,2,128]{3,0,2,1:T(8,128)(2,1)}), bf16[64,64,2,128]{3,0,2,1:T(8,128)(2,1)}) %all-gather.2.cloned.1.call-update) | async-done | bytes 2097168 | tf_op jit(solution)/shard_map/while/body/eval_jaxpr/all_gather | solution.py:40
  485.4 3.7 fusion.58
  489.1 7.0 collective-permute-start
  498.7 75.5 %all-gather.2.cloned.1.call-done = bf16[64,64,2,128]{3,0,2,1:T(8,128)(2,1)} async-done(((bf16[64,2,2,128]{3,0,2,1:T(8,128)(2,1)}), bf16[64,64,2,128]{3,0,2,1:T(8,128)(2,1)}) %all-gather.2.cloned.1.call-update) | async-done | bytes 2097168 | tf_op jit(solution)/shard_map/while/body/eval_jaxpr/all_gather | solution.py:40
  586.3 7.0 collective-permute-start
  596.0 75.8 %all-gather.2.cloned.1.call-done = bf16[64,64,2,128]{3,0,2,1:T(8,128)(2,1)} async-done(((bf16[64,2,2,128]{3,0,2,1:T(8,128)(2,1)}), bf16[64,64,2,128]{3,0,2,1:T(8,128)(2,1)}) %all-gather.2.cloned.1.call-update) | async-done | bytes 2097168 | tf_op jit(solution)/shard_map/while/body/eval_jaxpr/all_gather | solution.py:40
  683.8 7.0 collective-permute-start
  693.5 75.8 %all-gather.2.cloned.1.call-done = bf16[64,64,2,128]{3,0,2,1:T(8,128)(2,1)} async-done(((bf16[64,2,2,128]{3,0,2,1:T(8,128)(2,1)}), bf16[64,64,2,128]{3,0,2,1:T(8,128)(2,1)}) %all-gather.2.cloned.1.call-update) | async-done | bytes 2097168 | tf_op jit(solution)/shard_map/while/body/eval_jaxpr/all_gather | solution.py:40
  781.3 7.0 collective-permute-start
  790.4 4.4 collective-permute-start.1
  800.8 3.8 collective-permute-start.3
  806.9 6.4 collective-permute-done.4
  (162 shorter events, 112.6 us)
Async XLA Ops:
  8.1 788.5 %copy-start.2 = (f32[1,2,128]{2,1,0:T(2,128)S(1)}, f32[1,2,128]{2,1,0:T(2,128)}, u32[]{:S(2)}) copy-start(f32[1,2,128]{2,1,0:T(2,128)} %param.8) | copy-start | bytes 3076
  8.2 805.9 %copy-start.1 = (f32[1,64,2,2,128]{4,3,2,1,0:T(2,128)S(1)}, f32[1,64,2,2,128]{4,3,2,1,0:T(2,128)}, u32[]{:S(2)}) copy-start(f32[1,64,2,2,128]{4,3,2,1,0:T(2,128)} %param.6) | copy-start | bytes 393220
  8.2 79.5 %all-gather.2.cloned.1.call-start = ((), (), s32[]{:S(2)}) async-start(), calls=%async_computation | async-start | bytes 2162688 | tf_op jit(solution)/shard_map/while/body/eval_jaxpr/all_gather | solution.py:40
  99.8 8.9 %collective-permute-start = (f32[64,2,2,128]{3,1,0,2:T(2,128)S(1)}, f32[64,2,2,128]{3,1,0,2:T(2,128)S(1)}, u32[]{:S(2)}, u32[]{:S(2)}) collective-permute-start(f32[64,2,2,128]{3,1,0,2:T(2,128)S(1)} %constant_dynamic-update-slice_fusion.5), channel_id=1, source_target_pairs={{0,32},{32,64},{64,96},{96,128},{128,160},{160,192},{192,224},{1,3... | collective-permute-start | bytes 393224 | tf_op jit(solution)/shard_map/while/body/eval_jaxpr/ppermute | solution.py:10
  108.7 76.5 %all-gather.2.cloned.1.call-start = ((), (), s32[]{:S(2)}) async-start(), calls=%async_computation | async-start | bytes 2162688 | tf_op jit(solution)/shard_map/while/body/eval_jaxpr/all_gather | solution.py:40
  185.2 4.0 copy-start.3
  197.3 8.9 %collective-permute-start = (f32[64,2,2,128]{3,1,0,2:T(2,128)S(1)}, f32[64,2,2,128]{3,1,0,2:T(2,128)S(1)}, u32[]{:S(2)}, u32[]{:S(2)}) collective-permute-start(f32[64,2,2,128]{3,1,0,2:T(2,128)S(1)} %constant_dynamic-update-slice_fusion.5), channel_id=1, source_target_pairs={{0,32},{32,64},{64,96},{96,128},{128,160},{160,192},{192,224},{1,3... | collective-permute-start | bytes 393224 | tf_op jit(solution)/shard_map/while/body/eval_jaxpr/ppermute | solution.py:10
  206.2 76.5 %all-gather.2.cloned.1.call-start = ((), (), s32[]{:S(2)}) async-start(), calls=%async_computation | async-start | bytes 2162688 | tf_op jit(solution)/shard_map/while/body/eval_jaxpr/all_gather | solution.py:40
  294.8 8.9 %collective-permute-start = (f32[64,2,2,128]{3,1,0,2:T(2,128)S(1)}, f32[64,2,2,128]{3,1,0,2:T(2,128)S(1)}, u32[]{:S(2)}, u32[]{:S(2)}) collective-permute-start(f32[64,2,2,128]{3,1,0,2:T(2,128)S(1)} %constant_dynamic-update-slice_fusion.5), channel_id=1, source_target_pairs={{0,32},{32,64},{64,96},{96,128},{128,160},{160,192},{192,224},{1,3... | collective-permute-start | bytes 393224 | tf_op jit(solution)/shard_map/while/body/eval_jaxpr/ppermute | solution.py:10
  303.7 76.2 %all-gather.2.cloned.1.call-start = ((), (), s32[]{:S(2)}) async-start(), calls=%async_computation | async-start | bytes 2162688 | tf_op jit(solution)/shard_map/while/body/eval_jaxpr/all_gather | solution.py:40
  391.9 8.9 %collective-permute-start = (f32[64,2,2,128]{3,1,0,2:T(2,128)S(1)}, f32[64,2,2,128]{3,1,0,2:T(2,128)S(1)}, u32[]{:S(2)}, u32[]{:S(2)}) collective-permute-start(f32[64,2,2,128]{3,1,0,2:T(2,128)S(1)} %constant_dynamic-update-slice_fusion.5), channel_id=1, source_target_pairs={{0,32},{32,64},{64,96},{96,128},{128,160},{160,192},{192,224},{1,3... | collective-permute-start | bytes 393224 | tf_op jit(solution)/shard_map/while/body/eval_jaxpr/ppermute | solution.py:10
  400.9 76.2 %all-gather.2.cloned.1.call-start = ((), (), s32[]{:S(2)}) async-start(), calls=%async_computation | async-start | bytes 2162688 | tf_op jit(solution)/shard_map/while/body/eval_jaxpr/all_gather | solution.py:40
  489.1 8.9 %collective-permute-start = (f32[64,2,2,128]{3,1,0,2:T(2,128)S(1)}, f32[64,2,2,128]{3,1,0,2:T(2,128)S(1)}, u32[]{:S(2)}, u32[]{:S(2)}) collective-permute-start(f32[64,2,2,128]{3,1,0,2:T(2,128)S(1)} %constant_dynamic-update-slice_fusion.5), channel_id=1, source_target_pairs={{0,32},{32,64},{64,96},{96,128},{128,160},{160,192},{192,224},{1,3... | collective-permute-start | bytes 393224 | tf_op jit(solution)/shard_map/while/body/eval_jaxpr/ppermute | solution.py:10
  498.1 76.2 %all-gather.2.cloned.1.call-start = ((), (), s32[]{:S(2)}) async-start(), calls=%async_computation | async-start | bytes 2162688 | tf_op jit(solution)/shard_map/while/body/eval_jaxpr/all_gather | solution.py:40
  586.3 8.9 %collective-permute-start = (f32[64,2,2,128]{3,1,0,2:T(2,128)S(1)}, f32[64,2,2,128]{3,1,0,2:T(2,128)S(1)}, u32[]{:S(2)}, u32[]{:S(2)}) collective-permute-start(f32[64,2,2,128]{3,1,0,2:T(2,128)S(1)} %constant_dynamic-update-slice_fusion.5), channel_id=1, source_target_pairs={{0,32},{32,64},{64,96},{96,128},{128,160},{160,192},{192,224},{1,3... | collective-permute-start | bytes 393224 | tf_op jit(solution)/shard_map/while/body/eval_jaxpr/ppermute | solution.py:10
  595.2 76.5 %all-gather.2.cloned.1.call-start = ((), (), s32[]{:S(2)}) async-start(), calls=%async_computation | async-start | bytes 2162688 | tf_op jit(solution)/shard_map/while/body/eval_jaxpr/all_gather | solution.py:40
  683.8 8.9 %collective-permute-start = (f32[64,2,2,128]{3,1,0,2:T(2,128)S(1)}, f32[64,2,2,128]{3,1,0,2:T(2,128)S(1)}, u32[]{:S(2)}, u32[]{:S(2)}) collective-permute-start(f32[64,2,2,128]{3,1,0,2:T(2,128)S(1)} %constant_dynamic-update-slice_fusion.5), channel_id=1, source_target_pairs={{0,32},{32,64},{64,96},{96,128},{128,160},{160,192},{192,224},{1,3... | collective-permute-start | bytes 393224 | tf_op jit(solution)/shard_map/while/body/eval_jaxpr/ppermute | solution.py:10
  692.7 76.5 %all-gather.2.cloned.1.call-start = ((), (), s32[]{:S(2)}) async-start(), calls=%async_computation | async-start | bytes 2162688 | tf_op jit(solution)/shard_map/while/body/eval_jaxpr/all_gather | solution.py:40
  781.3 8.9 %collective-permute-start = (f32[64,2,2,128]{3,1,0,2:T(2,128)S(1)}, f32[64,2,2,128]{3,1,0,2:T(2,128)S(1)}, u32[]{:S(2)}, u32[]{:S(2)}) collective-permute-start(f32[64,2,2,128]{3,1,0,2:T(2,128)S(1)} %constant_dynamic-update-slice_fusion.5), channel_id=1, source_target_pairs={{0,32},{32,64},{64,96},{96,128},{128,160},{160,192},{192,224},{1,3... | collective-permute-start | bytes 393224 | tf_op jit(solution)/shard_map/while/body/eval_jaxpr/ppermute | solution.py:10
  790.4 24.5 %copy-start = (f32[1,64,2,2,128]{4,3,2,1,0:T(2,128)}, f32[1,64,2,2,128]{4,3,2,1,0:T(2,128)S(1)}, u32[]{:S(2)}) copy-start(f32[1,64,2,2,128]{4,3,2,1,0:T(2,128)S(1)} %get-tuple-element.170) | copy-start | bytes 393220
  790.4 7.0 collective-permute-start.1
  794.8 5.6 collective-permute-start.2
  800.8 6.1 collective-permute-start.3
  804.6 8.7 %collective-permute-start.4 = (bf16[3,64,1,2,128]{4,3,2,1,0:T(2,128)(2,1)S(1)}, bf16[3,64,1,2,128]{4,3,2,1,0:T(2,128)(2,1)S(1)}, u32[]{:S(2)}, u32[]{:S(2)}) collective-permute-start(bf16[3,64,1,2,128]{4,3,2,1,0:T(2,128)(2,1)S(1)} %get-tuple-element.176), channel_id=1, source_target_pairs={{1,0},{2,1},{3,2},{4,3},{5,4},{6,5},{7,6},{8,7},{9,8},{10,9},{11,1... | collective-permute-start | bytes 294920 | tf_op jit(solution)/shard_map/ppermute | solution.py:23
  (7 other events, 28.1 us)
Sparse Core Ops, SparseCore 0:
  12.2 75.4 all-gather.1
  112.7 72.5 all-gather.1
  210.2 72.5 all-gather.1
  307.3 72.5 all-gather.1
  404.5 72.5 all-gather.1
  501.7 72.5 all-gather.1
  599.2 72.5 all-gather.1
  696.7 72.5 all-gather.1
where the time goes:
time: 822 us
  waiting for transfers between devices  633 us (77%)
  starting transfers between devices  67.9 us (8%)
  matrix products  63.2 us (8%)
  local copies, waits for them, and re-layouts  33.8 us (4%)
  between operations  14.8 us (2%)
  other arithmetic  8.63 us (1%)
    all_gather x8, waiting for transfers between devices, apply_front(): vector_piece = lax.all_gather(combined, 'front', axis=1, tiled=True)  609 us
    ppermute x8, starting transfers between devices, from_behind(): return lax.ppermute(shard, axis, pairs)  55.9 us
    dot_general x8, matrix products, apply_front(): lax.dot_general(part_re, front_re, dims, preferred_element_type=jnp.float32)  29.3 us
    slice x16, local copies, waits for them, and re-layouts, apply_front(): part_re = vector_piece[:, :, 0].reshape(block_size, width)  20.5 us
  transfers between devices with their start and end apart: 20, of which 19 were waited for; matrix products, arithmetic and copies ran while one was open for 0% of the time, Pallas kernels for 0%

commit v1 on v0

--- a/solution.py
+++ b/solution.py
@@ -37,7 +37,9 @@
     def apply_front(combined, local_panel):
         front_re = fronts[local_panel, 0]
         front_im = fronts[local_panel, 1]
-        vector_piece = lax.all_gather(combined, "front", axis=1, tiled=True)
+        vector_piece = jnp.concatenate(
+            lax.all_to_all(jnp.stack([combined] * lax.axis_size("front")), "front", 0, 0), axis=1
+        )
         piece_rows = vector_piece.shape[1]
         width = piece_rows * columns
         part_re = vector_piece[:, :, 0].reshape(block_size, width)

time: 822 us -> 621 us (0.76)
  waiting for transfers between devices: 633 us -> 394 us
  starting transfers between devices: 67.9 us -> 108 us
  between operations: 14.8 us -> 1.42 us
  local copies, waits for them, and re-layouts: 33.8 us -> 43.8 us
    all_gather x8 -> x0, waiting for transfers between devices: 609 us -> none  [apply_front(): vector_piece = lax.all_gather(combined, 'front', axis=1, tiled=True)]
    all_to_all x0 -> x8, waiting for transfers between devices: none -> 372 us  [apply_front(): lax.all_to_all(jnp.stack([combined] * lax.axis_size('front')), 'front', 0...]
    all_to_all x0 -> x8, starting transfers between devices: none -> 50.1 us  [apply_front(): lax.all_to_all(jnp.stack([combined] * lax.axis_size('front')), 'front', 0...]
    another operation x0 -> x8, local copies, waits for them, and re-layouts: none -> 14.9 us  [apply_front(): jnp.stack([combined] * lax.axis_size('front'))]
    slice x16, local copies, waits for them, and re-layouts: 20.5 us -> 6.81 us  [apply_front(): part_re = vector_piece[:, :, 0].reshape(block_size, width)]
    ppermute x8, starting transfers between devices: 55.9 us -> 44.7 us  [from_behind(): return lax.ppermute(shard, axis, pairs)]
    while x24, local copies, waits for them, and re-layouts: 6.14 us -> 14.7 us
  transfers between devices with their start and end apart: 20 -> 20, of which waited for: 19 -> 18; matrix products, arithmetic and copies ran while one was open for 0% -> 0% of each run, Pallas kernels for 0% -> 0%
where the time goes in v1:
time: 621 us; the launch traced here: 615 us
  waiting for transfers between devices  394 us (63%)
  starting transfers between devices  108 us (17%)
  matrix products  63.2 us (10%)
  local copies, waits for them, and re-layouts  43.8 us (7%)
    all_to_all x8, waiting for transfers between devices, apply_front(): lax.all_to_all(jnp.stack([combined] * lax.axis_size('front')), 'front', 0...  372 us
    all_to_all x8, starting transfers between devices, apply_front(): lax.all_to_all(jnp.stack([combined] * lax.axis_size('front')), 'front', 0...  50.1 us
    ppermute x8, starting transfers between devices, from_behind(): return lax.ppermute(shard, axis, pairs)  44.7 us
    dot_general x8, matrix products, apply_front(): lax.dot_general(part_re, front_re, dims, preferred_element_type=jnp.float32)  29.3 us
    another operation x8, local copies, waits for them, and re-layouts, apply_front(): jnp.stack([combined] * lax.axis_size('front'))  14.9 us
    ppermute x8, waiting for transfers between devices, from_behind(): return lax.ppermute(shard, axis, pairs)  14.7 us
    while x24, local copies, waits for them, and re-layouts  14.7 us
  transfers between devices with their start and end apart: 20, of which 18 were waited for; matrix products, arithmetic and copies ran while one was open for 0% of the time, Pallas kernels for 0%

profile of v1, /device:TPU:29, one launch (start us, length us, event | category | flops | bytes accessed | tf_op | source)
XLA Modules:
  0.0 614.5 jit_solution(4500301320116646153)
XLA Ops:
  1.7 590.3 %while.16 = (s32[]{:T(128)}, f32[1,64,2,2,128]{4,2,1,3,0:T(2,128)S(1)}, f32[64,2,2,128]{3,1,0,2:T(2,128)S(1)}, s32[]{:T(128)}, f32[1,64,2,2,128]{4,2,1,3,0:T(2,1...) while((s32[]{:T(128)}, f32[1,64,2,2,128]{4,2,1,3,0:T(2,128)S(1)}, ...), condition=%wide.region_1.2_spmd.clone, body=%wide.region_0.1_spmd.clone.sunk | while | flops 1073905664 | bytes 73662688 | solution.py:77
  3.7 10.9 %all-to-all-start = ((bf16[32,64,2,2,128]{4,1,3,2,0:T(8,128)(2,1)}), bf16[32,64,2,2,128]{4,1,3,2,0:T(8,128)(2,1)S(1)}, u32[]{:S(2)}, u32[]{:S(2)}) async-start(bf16[32,64,2,2,128]{4,1,3,2,0:T(8,128)(2,1)} %stack.18), calls=%async_computation | async-start | bytes 4194304 | tf_op jit(solution)/shard_map/while/body/eval_jaxpr/all_to_all | solution.py:41
  14.6 50.4 %all-to-all-done = bf16[32,64,2,2,128]{4,1,3,2,0:T(8,128)(2,1)S(1)} async-done(((bf16[32,64,2,2,128]{4,1,3,2,0:T(8,128)(2,1)}), bf16[32,64,2,2,128]{4,1,3,2,0:T(8,128)(2,1)S(1)}, u32[]{:S(2)}, u32[]{:S(2)}) %all-to-all-start) | async-done | bytes 2097184 | tf_op jit(solution)/shard_map/while/body/eval_jaxpr/all_to_all | solution.py:41
  83.6 5.7 all-to-all-start
  89.4 49.2 %all-to-all-done = bf16[32,64,2,2,128]{4,1,3,2,0:T(8,128)(2,1)S(1)} async-done(((bf16[32,64,2,2,128]{4,1,3,2,0:T(8,128)(2,1)}), bf16[32,64,2,2,128]{4,1,3,2,0:T(8,128)(2,1)S(1)}, u32[]{:S(2)}, u32[]{:S(2)}) %all-to-all-start) | async-done | bytes 2097184 | tf_op jit(solution)/shard_map/while/body/eval_jaxpr/all_to_all | solution.py:41
  157.2 5.0 all-to-all-start
  162.3 45.4 %all-to-all-done = bf16[32,64,2,2,128]{4,1,3,2,0:T(8,128)(2,1)S(1)} async-done(((bf16[32,64,2,2,128]{4,1,3,2,0:T(8,128)(2,1)}), bf16[32,64,2,2,128]{4,1,3,2,0:T(8,128)(2,1)S(1)}, u32[]{:S(2)}, u32[]{:S(2)}) %all-to-all-start) | async-done | bytes 2097184 | tf_op jit(solution)/shard_map/while/body/eval_jaxpr/all_to_all | solution.py:41
  219.1 6.5 %collective-permute-start = (f32[64,2,2,128]{3,1,0,2:T(2,128)S(1)}, f32[64,2,2,128]{3,1,0,2:T(2,128)S(1)}, u32[]{:S(2)}, u32[]{:S(2)}) collective-permute-start(f32[64,2,2,128]{3,1,0,2:T(2,128)S(1)} %constant_dynamic-update-slice_fusion.5), channel_id=1, source_target_pairs={{0,32},{32,64},{64,96},{96,128},{128,160},{160,192},{192,224},{1,3... | collective-permute-start | bytes 393224 | tf_op jit(solution)/shard_map/while/body/eval_jaxpr/ppermute | solution.py:10
  229.5 5.7 all-to-all-start
  235.2 45.4 %all-to-all-done = bf16[32,64,2,2,128]{4,1,3,2,0:T(8,128)(2,1)S(1)} async-done(((bf16[32,64,2,2,128]{4,1,3,2,0:T(8,128)(2,1)}), bf16[32,64,2,2,128]{4,1,3,2,0:T(8,128)(2,1)S(1)}, u32[]{:S(2)}, u32[]{:S(2)}) %all-to-all-start) | async-done | bytes 2097184 | tf_op jit(solution)/shard_map/while/body/eval_jaxpr/all_to_all | solution.py:41
  292.0 6.5 %collective-permute-start = (f32[64,2,2,128]{3,1,0,2:T(2,128)S(1)}, f32[64,2,2,128]{3,1,0,2:T(2,128)S(1)}, u32[]{:S(2)}, u32[]{:S(2)}) collective-permute-start(f32[64,2,2,128]{3,1,0,2:T(2,128)S(1)} %constant_dynamic-update-slice_fusion.5), channel_id=1, source_target_pairs={{0,32},{32,64},{64,96},{96,128},{128,160},{160,192},{192,224},{1,3... | collective-permute-start | bytes 393224 | tf_op jit(solution)/shard_map/while/body/eval_jaxpr/ppermute | solution.py:10
  302.3 5.7 all-to-all-start
  308.1 45.4 %all-to-all-done = bf16[32,64,2,2,128]{4,1,3,2,0:T(8,128)(2,1)S(1)} async-done(((bf16[32,64,2,2,128]{4,1,3,2,0:T(8,128)(2,1)}), bf16[32,64,2,2,128]{4,1,3,2,0:T(8,128)(2,1)S(1)}, u32[]{:S(2)}, u32[]{:S(2)}) %all-to-all-start) | async-done | bytes 2097184 | tf_op jit(solution)/shard_map/while/body/eval_jaxpr/all_to_all | solution.py:41
  364.9 6.5 %collective-permute-start = (f32[64,2,2,128]{3,1,0,2:T(2,128)S(1)}, f32[64,2,2,128]{3,1,0,2:T(2,128)S(1)}, u32[]{:S(2)}, u32[]{:S(2)}) collective-permute-start(f32[64,2,2,128]{3,1,0,2:T(2,128)S(1)} %constant_dynamic-update-slice_fusion.5), channel_id=1, source_target_pairs={{0,32},{32,64},{64,96},{96,128},{128,160},{160,192},{192,224},{1,3... | collective-permute-start | bytes 393224 | tf_op jit(solution)/shard_map/while/body/eval_jaxpr/ppermute | solution.py:10
  375.2 5.7 all-to-all-start
  381.0 45.4 %all-to-all-done = bf16[32,64,2,2,128]{4,1,3,2,0:T(8,128)(2,1)S(1)} async-done(((bf16[32,64,2,2,128]{4,1,3,2,0:T(8,128)(2,1)}), bf16[32,64,2,2,128]{4,1,3,2,0:T(8,128)(2,1)S(1)}, u32[]{:S(2)}, u32[]{:S(2)}) %all-to-all-start) | async-done | bytes 2097184 | tf_op jit(solution)/shard_map/while/body/eval_jaxpr/all_to_all | solution.py:41
  437.8 6.5 %collective-permute-start = (f32[64,2,2,128]{3,1,0,2:T(2,128)S(1)}, f32[64,2,2,128]{3,1,0,2:T(2,128)S(1)}, u32[]{:S(2)}, u32[]{:S(2)}) collective-permute-start(f32[64,2,2,128]{3,1,0,2:T(2,128)S(1)} %constant_dynamic-update-slice_fusion.5), channel_id=1, source_target_pairs={{0,32},{32,64},{64,96},{96,128},{128,160},{160,192},{192,224},{1,3... | collective-permute-start | bytes 393224 | tf_op jit(solution)/shard_map/while/body/eval_jaxpr/ppermute | solution.py:10
  448.1 5.7 all-to-all-start
  453.8 45.4 %all-to-all-done = bf16[32,64,2,2,128]{4,1,3,2,0:T(8,128)(2,1)S(1)} async-done(((bf16[32,64,2,2,128]{4,1,3,2,0:T(8,128)(2,1)}), bf16[32,64,2,2,128]{4,1,3,2,0:T(8,128)(2,1)S(1)}, u32[]{:S(2)}, u32[]{:S(2)}) %all-to-all-start) | async-done | bytes 2097184 | tf_op jit(solution)/shard_map/while/body/eval_jaxpr/all_to_all | solution.py:41
  510.7 6.5 %collective-permute-start = (f32[64,2,2,128]{3,1,0,2:T(2,128)S(1)}, f32[64,2,2,128]{3,1,0,2:T(2,128)S(1)}, u32[]{:S(2)}, u32[]{:S(2)}) collective-permute-start(f32[64,2,2,128]{3,1,0,2:T(2,128)S(1)} %constant_dynamic-update-slice_fusion.5), channel_id=1, source_target_pairs={{0,32},{32,64},{64,96},{96,128},{128,160},{160,192},{192,224},{1,3... | collective-permute-start | bytes 393224 | tf_op jit(solution)/shard_map/while/body/eval_jaxpr/ppermute | solution.py:10
  521.0 5.7 all-to-all-start
  526.7 45.4 %all-to-all-done = bf16[32,64,2,2,128]{4,1,3,2,0:T(8,128)(2,1)S(1)} async-done(((bf16[32,64,2,2,128]{4,1,3,2,0:T(8,128)(2,1)}), bf16[32,64,2,2,128]{4,1,3,2,0:T(8,128)(2,1)S(1)}, u32[]{:S(2)}, u32[]{:S(2)}) %all-to-all-start) | async-done | bytes 2097184 | tf_op jit(solution)/shard_map/while/body/eval_jaxpr/all_to_all | solution.py:41
  583.6 6.5 %collective-permute-start = (f32[64,2,2,128]{3,1,0,2:T(2,128)S(1)}, f32[64,2,2,128]{3,1,0,2:T(2,128)S(1)}, u32[]{:S(2)}, u32[]{:S(2)}) collective-permute-start(f32[64,2,2,128]{3,1,0,2:T(2,128)S(1)} %constant_dynamic-update-slice_fusion.5), channel_id=1, source_target_pairs={{0,32},{32,64},{64,96},{96,128},{128,160},{160,192},{192,224},{1,3... | collective-permute-start | bytes 393224 | tf_op jit(solution)/shard_map/while/body/eval_jaxpr/ppermute | solution.py:10
  607.9 5.0 collective-permute-done.4
  (170 shorter events, 146.3 us)
Async XLA Ops:
  1.7 597.8 %copy-start.2 = (f32[1,2,128]{2,1,0:T(2,128)S(1)}, f32[1,2,128]{2,1,0:T(2,128)}, u32[]{:S(2)}) copy-start(f32[1,2,128]{2,1,0:T(2,128)} %param.8) | copy-start | bytes 3076
  1.7 612.0 %copy-start.1 = (f32[1,64,2,2,128]{4,3,2,1,0:T(2,128)S(1)}, f32[1,64,2,2,128]{4,3,2,1,0:T(2,128)}, u32[]{:S(2)}) copy-start(f32[1,64,2,2,128]{4,3,2,1,0:T(2,128)} %param.6) | copy-start | bytes 393220
  3.7 61.4 %all-to-all-start = ((bf16[32,64,2,2,128]{4,1,3,2,0:T(8,128)(2,1)}), bf16[32,64,2,2,128]{4,1,3,2,0:T(8,128)(2,1)S(1)}, u32[]{:S(2)}, u32[]{:S(2)}) async-start(bf16[32,64,2,2,128]{4,1,3,2,0:T(8,128)(2,1)} %stack.18), calls=%async_computation | async-start | bytes 4194304 | tf_op jit(solution)/shard_map/while/body/eval_jaxpr/all_to_all | solution.py:41
  76.4 5.2 collective-permute-start
  83.6 55.0 %all-to-all-start = ((bf16[32,64,2,2,128]{4,1,3,2,0:T(8,128)(2,1)}), bf16[32,64,2,2,128]{4,1,3,2,0:T(8,128)(2,1)S(1)}, u32[]{:S(2)}, u32[]{:S(2)}) async-start(bf16[32,64,2,2,128]{4,1,3,2,0:T(8,128)(2,1)} %stack.18), calls=%async_computation | async-start | bytes 4194304 | tf_op jit(solution)/shard_map/while/body/eval_jaxpr/all_to_all | solution.py:41
  150.0 5.3 collective-permute-start
  157.2 50.5 %all-to-all-start = ((bf16[32,64,2,2,128]{4,1,3,2,0:T(8,128)(2,1)}), bf16[32,64,2,2,128]{4,1,3,2,0:T(8,128)(2,1)S(1)}, u32[]{:S(2)}, u32[]{:S(2)}) async-start(bf16[32,64,2,2,128]{4,1,3,2,0:T(8,128)(2,1)} %stack.18), calls=%async_computation | async-start | bytes 4194304 | tf_op jit(solution)/shard_map/while/body/eval_jaxpr/all_to_all | solution.py:41
  219.1 8.4 %collective-permute-start = (f32[64,2,2,128]{3,1,0,2:T(2,128)S(1)}, f32[64,2,2,128]{3,1,0,2:T(2,128)S(1)}, u32[]{:S(2)}, u32[]{:S(2)}) collective-permute-start(f32[64,2,2,128]{3,1,0,2:T(2,128)S(1)} %constant_dynamic-update-slice_fusion.5), channel_id=1, source_target_pairs={{0,32},{32,64},{64,96},{96,128},{128,160},{160,192},{192,224},{1,3... | collective-permute-start | bytes 393224 | tf_op jit(solution)/shard_map/while/body/eval_jaxpr/ppermute | solution.py:10
  229.5 51.1 %all-to-all-start = ((bf16[32,64,2,2,128]{4,1,3,2,0:T(8,128)(2,1)}), bf16[32,64,2,2,128]{4,1,3,2,0:T(8,128)(2,1)S(1)}, u32[]{:S(2)}, u32[]{:S(2)}) async-start(bf16[32,64,2,2,128]{4,1,3,2,0:T(8,128)(2,1)} %stack.18), calls=%async_computation | async-start | bytes 4194304 | tf_op jit(solution)/shard_map/while/body/eval_jaxpr/all_to_all | solution.py:41
  292.0 8.4 %collective-permute-start = (f32[64,2,2,128]{3,1,0,2:T(2,128)S(1)}, f32[64,2,2,128]{3,1,0,2:T(2,128)S(1)}, u32[]{:S(2)}, u32[]{:S(2)}) collective-permute-start(f32[64,2,2,128]{3,1,0,2:T(2,128)S(1)} %constant_dynamic-update-slice_fusion.5), channel_id=1, source_target_pairs={{0,32},{32,64},{64,96},{96,128},{128,160},{160,192},{192,224},{1,3... | collective-permute-start | bytes 393224 | tf_op jit(solution)/shard_map/while/body/eval_jaxpr/ppermute | solution.py:10
  302.3 51.1 %all-to-all-start = ((bf16[32,64,2,2,128]{4,1,3,2,0:T(8,128)(2,1)}), bf16[32,64,2,2,128]{4,1,3,2,0:T(8,128)(2,1)S(1)}, u32[]{:S(2)}, u32[]{:S(2)}) async-start(bf16[32,64,2,2,128]{4,1,3,2,0:T(8,128)(2,1)} %stack.18), calls=%async_computation | async-start | bytes 4194304 | tf_op jit(solution)/shard_map/while/body/eval_jaxpr/all_to_all | solution.py:41
  364.9 8.4 %collective-permute-start = (f32[64,2,2,128]{3,1,0,2:T(2,128)S(1)}, f32[64,2,2,128]{3,1,0,2:T(2,128)S(1)}, u32[]{:S(2)}, u32[]{:S(2)}) collective-permute-start(f32[64,2,2,128]{3,1,0,2:T(2,128)S(1)} %constant_dynamic-update-slice_fusion.5), channel_id=1, source_target_pairs={{0,32},{32,64},{64,96},{96,128},{128,160},{160,192},{192,224},{1,3... | collective-permute-start | bytes 393224 | tf_op jit(solution)/shard_map/while/body/eval_jaxpr/ppermute | solution.py:10
  375.2 51.1 %all-to-all-start = ((bf16[32,64,2,2,128]{4,1,3,2,0:T(8,128)(2,1)}), bf16[32,64,2,2,128]{4,1,3,2,0:T(8,128)(2,1)S(1)}, u32[]{:S(2)}, u32[]{:S(2)}) async-start(bf16[32,64,2,2,128]{4,1,3,2,0:T(8,128)(2,1)} %stack.18), calls=%async_computation | async-start | bytes 4194304 | tf_op jit(solution)/shard_map/while/body/eval_jaxpr/all_to_all | solution.py:41
  426.4 3.4 copy-start.3
  437.8 8.4 %collective-permute-start = (f32[64,2,2,128]{3,1,0,2:T(2,128)S(1)}, f32[64,2,2,128]{3,1,0,2:T(2,128)S(1)}, u32[]{:S(2)}, u32[]{:S(2)}) collective-permute-start(f32[64,2,2,128]{3,1,0,2:T(2,128)S(1)} %constant_dynamic-update-slice_fusion.5), channel_id=1, source_target_pairs={{0,32},{32,64},{64,96},{96,128},{128,160},{160,192},{192,224},{1,3... | collective-permute-start | bytes 393224 | tf_op jit(solution)/shard_map/while/body/eval_jaxpr/ppermute | solution.py:10
  448.1 51.1 %all-to-all-start = ((bf16[32,64,2,2,128]{4,1,3,2,0:T(8,128)(2,1)}), bf16[32,64,2,2,128]{4,1,3,2,0:T(8,128)(2,1)S(1)}, u32[]{:S(2)}, u32[]{:S(2)}) async-start(bf16[32,64,2,2,128]{4,1,3,2,0:T(8,128)(2,1)} %stack.18), calls=%async_computation | async-start | bytes 4194304 | tf_op jit(solution)/shard_map/while/body/eval_jaxpr/all_to_all | solution.py:41
  510.7 8.4 %collective-permute-start = (f32[64,2,2,128]{3,1,0,2:T(2,128)S(1)}, f32[64,2,2,128]{3,1,0,2:T(2,128)S(1)}, u32[]{:S(2)}, u32[]{:S(2)}) collective-permute-start(f32[64,2,2,128]{3,1,0,2:T(2,128)S(1)} %constant_dynamic-update-slice_fusion.5), channel_id=1, source_target_pairs={{0,32},{32,64},{64,96},{96,128},{128,160},{160,192},{192,224},{1,3... | collective-permute-start | bytes 393224 | tf_op jit(solution)/shard_map/while/body/eval_jaxpr/ppermute | solution.py:10
  521.0 51.1 %all-to-all-start = ((bf16[32,64,2,2,128]{4,1,3,2,0:T(8,128)(2,1)}), bf16[32,64,2,2,128]{4,1,3,2,0:T(8,128)(2,1)S(1)}, u32[]{:S(2)}, u32[]{:S(2)}) async-start(bf16[32,64,2,2,128]{4,1,3,2,0:T(8,128)(2,1)} %stack.18), calls=%async_computation | async-start | bytes 4194304 | tf_op jit(solution)/shard_map/while/body/eval_jaxpr/all_to_all | solution.py:41
  583.6 8.4 %collective-permute-start = (f32[64,2,2,128]{3,1,0,2:T(2,128)S(1)}, f32[64,2,2,128]{3,1,0,2:T(2,128)S(1)}, u32[]{:S(2)}, u32[]{:S(2)}) collective-permute-start(f32[64,2,2,128]{3,1,0,2:T(2,128)S(1)} %constant_dynamic-update-slice_fusion.5), channel_id=1, source_target_pairs={{0,32},{32,64},{64,96},{96,128},{128,160},{160,192},{192,224},{1,3... | collective-permute-start | bytes 393224 | tf_op jit(solution)/shard_map/while/body/eval_jaxpr/ppermute | solution.py:10
  592.1 22.4 %copy-start = (f32[1,64,2,2,128]{4,3,2,1,0:T(2,128)}, f32[1,64,2,2,128]{4,3,2,1,0:T(2,128)S(1)}, u32[]{:S(2)}) copy-start(f32[1,64,2,2,128]{4,3,2,1,0:T(2,128)S(1)} %get-tuple-element.162) | copy-start | bytes 393220
  592.1 8.1 %collective-permute-start.1 = (bf16[1,64,2,2,128]{4,3,2,1,0:T(2,128)(2,1)S(1)}, bf16[1,64,2,2,128]{4,3,2,1,0:T(2,128)(2,1)S(1)}, u32[]{:S(2)}, u32[]{:S(2)}) collective-permute-start(bf16[1,64,2,2,128]{4,3,2,1,0:T(2,128)(2,1)S(1)} %get-tuple-element.161), channel_id=1, source_target_pairs={{0,32},{32,64},{64,96},{96,128},{128,160},{160,192},{192,224},{1,3... | collective-permute-start | bytes 196616 | tf_op jit(solution)/shard_map/ppermute | solution.py:21
  596.5 5.6 collective-permute-start.2
  602.5 5.4 collective-permute-start.3
  605.4 7.5 %collective-permute-start.4 = (bf16[3,64,1,2,128]{4,3,2,1,0:T(2,128)(2,1)S(1)}, bf16[3,64,1,2,128]{4,3,2,1,0:T(2,128)(2,1)S(1)}, u32[]{:S(2)}, u32[]{:S(2)}) collective-permute-start(bf16[3,64,1,2,128]{4,3,2,1,0:T(2,128)(2,1)S(1)} %get-tuple-element.168), channel_id=1, source_target_pairs={{1,0},{2,1},{3,2},{4,3},{5,4},{6,5},{7,6},{8,7},{9,8},{10,9},{11,1... | collective-permute-start | bytes 294920 | tf_op jit(solution)/shard_map/ppermute | solution.py:23
  (7 other events, 23.7 us)
